TPU v7x, 32 devices: a whole 2x2x4 slice. The times are simulated.
32 devices in a mesh: groups: 2 (over x), ctx: 16 (over z, y, core).
Axes of the slice: x: 2, y: 2, z: 4, core: 2. Of those that a mesh axis runs over, the one named last changes fastest.
Arguments:
- key_cache: bfloat16 [4, 16384, 128], P(None, ('groups', 'ctx')), parts along dimension 1, may hold values from -16 to 16
- value_cache: bfloat16 [4, 16384, 128], P(None, ('groups', 'ctx')), parts along dimension 1, may hold values from -6 to 6
- init_centroids: bfloat16 [4, 1024, 128], replicated, may hold values from -6 to 6
- block_clusters: int32 [4, 128], P(None, 'groups'), parts along dimension 1, may hold values from 0 to 1023, as said below
- chosen_clusters: int32 [16, 4, 32], P('groups'), parts along dimension 0, may hold values from 0 to 1023, as said below
- request_positions: int32 [16], P('groups'), parts along dimension 0, may hold values from 1 to 8192, as said below
- queries: bfloat16 [16, 4, 8, 128], P('groups'), parts along dimension 0, may hold values from -640 to 640
Outputs:
- centroids: float32 [4, 2048, 128], P(None, ('groups', 'ctx')), parts along dimension 1
- attended: bfloat16 [16, 4, 8, 128], P('groups'), parts along dimension 0
There are 2 independent parts, one for each index of `groups`. A program takes and returns all parts, laid end to end along the dimension named above; an argument that names none is the same for every part. Nothing has to cross between parts.
Inputs may be any that keep to these rules, and one draw needn't show every extreme that they name: `block_clusters`: the owner of cluster c is the ctx index c // 64. Over the 4 x 4 pairs (head, block) of one device's blocks, at most 2 pairs have clusters of one owner; 2 owners get exactly 2 pairs from every device. `chosen_clusters`: the 32 clusters of one request and head are distinct. `request_positions`: at least half of the requests see all 8192 tokens.
All inputs are finite; a program needn't handle non-finite values.
Results may differ from a plain program's by a relative error of at most 0.0078.
Values may be sent and summed in bfloat16 or wider, within the bound.
A program may use at most 64 MiB of HBM per device.

v0:
```python
import functools
import math

import jax
import jax.numpy as jnp
from jax import lax
from jax.experimental import pallas as pl
from jax.experimental.pallas import tpu as pltpu
from jax.sharding import PartitionSpec as P

BLOCK = 128
SHARPNESS = 16.0
EPSILON = 1e-06
NEGATIVE = -1e30
MESH = pl.DeviceIdType.MESH
NT = (((1,), (1,)), ((), ()))
NN = (((1,), (0,)), ((), ()))


def to_unit(vectors):
    vectors = vectors.astype(jnp.float32)
    return (
        vectors
        * lax.rsqrt(jnp.mean(vectors * vectors, axis=-1, keepdims=True) + EPSILON)
        * vectors.shape[-1] ** (-0.5)
    )


def flipped(index, bits):
    bit = 1
    while bit <= bits:
        if bits & bit:
            index = index + bit * (1 - 2 * ((index // bit) % 2))
        bit *= 2
    return index


def dot(a, b, dims, precision=None):
    return lax.dot_general(a, b, dims, preferred_element_type=jnp.float32, precision=precision)


def kernel(
    n,
    tile,
    key_hbm, value_hbm, init_hbm, queries_ref, chosen_ref, blocks_ref, positions_ref,
    cent_out, att_out,
    init_v, keys, units, values, cents, held, sums, sums_k, sums_v, mass_acc, mass,
    first_a, first_half, first_b, keys_a, vals_a, mass_a, keys_half, vals_half, mass_half,
    keys_b, vals_b, mass_b, unit_cents, cent_in, parts, fin, att,
    local_sem, k_send, k_recv, v_send, v_recv, a_send, a_recv, b_send, b_recv,
    g_send, g_recv, c_send, c_recv, f_send, f_recv, o_send, o_recv,
):
    heads, tok_dev, dim = key_hbm.shape
    requests, _, group, _ = queries_ref.shape
    rows = requests * group
    members = n // heads
    chips = members // 2
    share = cents.shape[1]
    owned = share // heads
    tiles = tok_dev // tile
    clusters = members * share
    pieces, piece_rows = att.shape[1], att.shape[2]
    me = lax.axis_index("ctx")
    head, core, chip = (me // 2) % heads, me % 2, me // (2 * heads)
    member = chip * 2 + core
    other = 1 - core

    def at(of_head, of_member):
        return (of_member // 2) * (2 * heads) + of_head * 2 + of_member % 2


    barrier = pltpu.get_barrier_semaphore()
    for step in range(1, n):
        pl.semaphore_signal(
            barrier, inc=1, device_id={"ctx": (me + step) % n}, device_id_type=MESH
        )

    def remote(src, dst, send, recv, target):
        return pltpu.make_async_remote_copy(
            src_ref=src, dst_ref=dst, send_sem=send, recv_sem=recv,
            device_id={"ctx": target}, device_id_type=MESH,
        )

    init_copy = pltpu.make_async_copy(init_hbm.at[head], init_v, local_sem.at[0])
    key_copy = pltpu.make_async_copy(key_hbm.at[head], keys.at[0], local_sem.at[1])
    value_copy = pltpu.make_async_copy(value_hbm.at[head], values.at[0], local_sem.at[2])
    init_copy.start()
    key_copy.start()
    value_copy.start()
    pl.semaphore_wait(barrier, n - 1)

    key_sends, value_sends = [], []
    for k in range(1, heads):
        to = flipped(head, k)
        key_sends.append(
            remote(key_hbm.at[to], keys.at[k], k_send.at[k], k_recv.at[k], at(to, member))
        )
        key_sends[-1].start()
    for k in range(1, heads):
        to = flipped(head, k)
        value_sends.append(
            remote(value_hbm.at[to], values.at[k], v_send.at[k], v_recv.at[k], at(to, member))
        )
        value_sends[-1].start()

    init_copy.wait()
    start = to_unit(init_v[...]).reshape(chips, heads, 2, owned, dim)
    for part in range(members):
        cents[part] = jnp.concatenate(
            [start[part // 2, s, part % 2] for s in range(heads)], axis=0
        ).astype(jnp.bfloat16)

    def weights_of(unit_keys, current):
        cosine = dot(current, unit_keys, NT)
        raised = jnp.exp2(cosine * (SHARPNESS * math.log2(math.e)))
        return raised * (1.0 / jnp.sum(raised, axis=0, keepdims=True))

    def scatter(stage, part, buffers, between=None):
        starts, halves, own = [], [], []
        for d in range(chips):
            place = (chip + d + 1) % chips
            for index, (term, (mine, came, _, _)) in enumerate(zip(part(place, other), buffers)):
                mine[place, other] = term
                starts.append(
                    remote(
                        mine.at[place, other], came.at[d], a_send.at[stage + index, d],
                        a_recv.at[stage + index, d], partner,
                    )
                )
                starts[-1].start()
            if between is not None and d == 0:
                between()
            for index, (term, (_, came, half, slots)) in enumerate(zip(part(place, core), buffers)):
                starts[d * len(buffers) + index].wait_recv()
                if d == chips - 1:
                    own.append(term + came[d])
                    continue
                half[d] = (term + came[d]).astype(half.dtype)
                halves.append(
                    remote(
                        half.at[d], slots.at[d], b_send.at[stage + index, d],
                        b_recv.at[stage + index, d], at(head, place * 2 + core),
                    )
                )
                halves[-1].start()
        return own, starts, halves

    def arrived(own, halves, slots, index, count):
        for d in range(chips - 1):
            halves[d * count + index].wait_recv()
            own = own + slots[d].astype(jnp.float32)
        return own

    partner = me + 1 - 2 * core

    key_copy.wait()
    for k in range(heads):
        if k:
            key_sends[k - 1].wait_recv()
        unit = to_unit(keys[k]).astype(jnp.bfloat16)
        for j in range(tiles):
            units[k * tiles + j] = unit[j * tile : (j + 1) * tile]
        current = cents[...].reshape(clusters, dim)
        total = None
        for j in range(tiles):
            w = weights_of(unit[j * tile : (j + 1) * tile], current).astype(jnp.bfloat16)
            if k == heads - 1:
                held[j] = w.reshape(members, share, tile)
                continue
            term = dot(w, keys[k, j * tile : (j + 1) * tile], NN)
            total = term if total is None else total + term
        if k < heads - 1:
            total = total.reshape(chips, 2, share, dim)
            sums[...] = total if k == 0 else sums[...] + total

    def first_part(place, side):
        total = sums[place, side]
        for j in range(tiles):
            total = total + dot(
                held[j, place * 2 + side], keys[heads - 1, j * tile : (j + 1) * tile], NN
            )
        return (total,)

    (own,), first_starts, first_halves = scatter(
        0, first_part, ((sums, first_a, first_half, first_b),)
    )

    own = arrived(own, first_halves, first_b, 0, 1)
    unit_cents[member] = to_unit(own).astype(jnp.bfloat16)
    gathers = []

    def share_out(place, index, target):
        piece = unit_cents.at[place]
        gathers.append(remote(piece, piece, g_send.at[index], g_recv.at[index], target))
        gathers[-1].start()

    for d in range(1, chips):
        share_out(member, d, at(head, (chip + d) % chips * 2 + core))
    share_out(member, chips, partner)

    row_ids = lax.broadcasted_iota(jnp.int32, (rows, 1), 0)
    seen = jnp.zeros((rows, 1), jnp.int32)
    for r in range(requests):
        seen = jnp.where(row_ids // group == r, positions_ref[r], seen)
    chosen = chosen_ref[:, 0, :]
    for s in range(1, heads):
        chosen = jnp.where(head == s, chosen_ref[:, s, :], chosen)
    ksel = chosen.shape[1]
    chosen = jnp.broadcast_to(chosen[:, None, :], (requests, group, ksel)).reshape(rows, ksel)
    query = queries_ref[:, head].astype(jnp.float32).reshape(rows, dim).astype(jnp.bfloat16)
    scale = dim ** (-0.5)
    lanes = lax.broadcasted_iota(jnp.int32, (rows, BLOCK), 1)

    def exact_scores():
        found = []
        for k in range(heads):
            device = at(flipped(head, k), member)
            score = dot(query, keys[k], NT) * scale
            for b in range(tok_dev // BLOCK):
                cluster = blocks_ref[head, device * (tok_dev // BLOCK) + b]
                hits = jnp.max(jnp.where(chosen == cluster, 1, 0), axis=1, keepdims=True) > 0
                place = device * tok_dev + b * BLOCK + lanes
                usable = hits & (place < seen)
                found.append(
                    jnp.where(usable, score[:, b * BLOCK : (b + 1) * BLOCK], NEGATIVE)
                )
        return jnp.concatenate(found, axis=1)

    exact = exact_scores()
    exact_peak = jnp.max(exact, axis=1, keepdims=True)
    exact_prob = jnp.where(exact > 0.5 * NEGATIVE, jnp.exp(exact - exact_peak), 0.0).astype(
        jnp.bfloat16
    )
    exact_sum = jnp.sum(exact_prob.astype(jnp.float32), axis=1, keepdims=True)
    lane_ids = lax.broadcasted_iota(jnp.int32, (rows, share), 1)
    cluster_ids = at(lane_ids // owned, member) * owned + lane_ids % owned
    picked = chosen[:, 0:1] == cluster_ids
    for k in range(1, ksel):
        picked = picked | (chosen[:, k : k + 1] == cluster_ids)
    picked = jnp.where(picked, 1.0, 0.0)

    for d in range(1, chips):
        place = (chip + chips - d) % chips * 2 + core
        piece = unit_cents.at[place]
        remote(piece, piece, g_send.at[d], g_recv.at[d], partner).wait_recv()
        share_out(place, chips + d, partner)
    for d in range(chips):
        place = (chip + chips - d) % chips * 2 + other
        piece = unit_cents.at[place]
        remote(piece, piece, g_send.at[chips + d], g_recv.at[chips + d], partner).wait_recv()

    def second(k, light):
        current = unit_cents[...].reshape(clusters, dim)
        for j in range(tiles):
            w = weights_of(units[k * tiles + j], current)
            held[k * tiles + j] = w.astype(jnp.bfloat16).reshape(members, share, tile)
            for lane in range(0, tile, BLOCK):
                piece = w[:, lane : lane + BLOCK].reshape(members, share, BLOCK)
                mass_acc[...] += piece
        return light

    mass_acc[...] = jnp.zeros_like(mass_acc)
    lax.fori_loop(0, heads, second, 0)
    ones = jnp.ones((8, BLOCK), jnp.float32)
    for part in range(members):
        mass[part // 2, part % 2] = dot(ones, mass_acc[part], NT, lax.Precision.HIGHEST)
    value_copy.wait()
    for copy in value_sends:
        copy.wait_recv()

    def mass_part(place, side):
        return (mass[place, side],)

    def second_part(place, side):
        total = None
        for k in range(heads):
            for j in range(tiles):
                span = slice(j * tile, (j + 1) * tile)
                both = jnp.concatenate([keys[k, span], values[k, span]], axis=1)
                term = dot(held[k * tiles + j, place * 2 + side], both, NN)
                total = term if total is None else total + term
        return (total[:, :dim], total[:, dim:])

    mass_starts = []
    for d in range(1, chips + 1):
        place = (chip + d) % chips
        mass_starts.append(
            remote(
                mass.at[place, other], mass_a.at[d - 1], a_send.at[3, d - 1], a_recv.at[3, d - 1],
                partner,
            )
        )
        mass_starts[-1].start()
    mass_halves, mass_own = [], []

    def pass_masses():
        for d in range(1, chips + 1):
            place = (chip + d) % chips
            mass_starts[d - 1].wait_recv()
            total = mass[place, core] + mass_a[d - 1]
            if d == chips:
                mass_own.append(total)
                continue
            mass_half[d - 1] = total
            mass_halves.append(
                remote(
                    mass_half.at[d - 1], mass_b.at[d - 1], b_send.at[3, d - 1], b_recv.at[3, d - 1],
                    at(head, place * 2 + core),
                )
            )
            mass_halves[-1].start()

    (own_keys, own_values), second_starts, second_halves = scatter(
        1, second_part, ((sums_k, keys_a, keys_half, keys_b), (sums_v, vals_a, vals_half, vals_b)),
        pass_masses,
    )
    exact_weighted = dot(exact_prob, values[...].reshape(heads * tok_dev, dim), NN)
    own_keys = arrived(own_keys, second_halves, keys_b, 0, 2)
    cent_in[head] = to_unit(own_keys).reshape(heads, owned, dim)
    cent_sends = []
    for k in range(1, heads):
        to = flipped(head, k)
        cent_sends.append(
            remote(
                cent_in.at[head, to], cent_in.at[heads, k], c_send.at[k], c_recv.at[k],
                at(to, member),
            )
        )
        cent_sends[-1].start()
    own_mass = arrived(mass_own[0], mass_halves, mass_b, 0, 1)

    mass_row = own_mass[0:1]
    eye = lax.broadcasted_iota(jnp.int32, (share, share), 0) == lax.broadcasted_iota(
        jnp.int32, (share, share), 1
    )
    mass_column = jnp.sum(jnp.where(eye, mass_row, 0.0), axis=1, keepdims=True)
    mean_keys = (own_keys / mass_column).astype(jnp.bfloat16)
    score = dot(query, mean_keys, NT) * scale + jnp.log(mass_row)
    usable = picked < 0.5
    score = jnp.where(usable, score, NEGATIVE)
    peak = jnp.maximum(jnp.max(score, axis=1, keepdims=True), exact_peak)
    prob = jnp.where(usable, jnp.exp(score - peak), 0.0).astype(jnp.bfloat16)
    exact_factor = jnp.exp(exact_peak - peak)
    weight_sum = jnp.sum(prob.astype(jnp.float32), axis=1, keepdims=True) + exact_sum * exact_factor
    own_values = arrived(own_values, second_halves, vals_b, 1, 2)
    mean_values = (own_values / mass_column).astype(jnp.bfloat16)
    weighted = dot(prob, mean_values, NN) + exact_weighted * exact_factor
    shape = (pieces, piece_rows, dim)
    parts[:, 0] = weighted.reshape(shape)
    parts[:, 1] = jnp.broadcast_to(weight_sum, (rows, dim)).reshape(shape)
    parts[:, 2] = jnp.broadcast_to(peak, (rows, dim)).reshape(shape)

    def holds(index, action):
        if pieces == members:
            action()
        else:
            pl.when(index < pieces)(action)

    for d in range(1, members):
        to = (member + d) % members

        def give(to=to, d=d):
            remote(parts.at[to], fin.at[d], f_send.at[d], f_recv.at[d], at(head, to)).start()

        holds(to, give)

    def finish():
        for d in range(1, members):
            remote(parts.at[0], fin.at[d], f_send.at[d], f_recv.at[d], partner).wait_recv()
        stats = [parts[member]] + [fin[d] for d in range(1, members)]
        top = stats[0][2]
        for stat in stats[1:]:
            top = jnp.maximum(top, stat[2])
        upper, lower = 0.0, 0.0
        for stat in stats:
            factor = jnp.exp(stat[2] - top)
            upper = upper + stat[0] * factor
            lower = lower + stat[1] * factor
        att[head, member] = (upper / lower).astype(jnp.bfloat16)
        for d in range(1, n):
            to = (me + d) % n
            remote(
                att.at[head, member], att.at[head, member], o_send.at[d], o_recv.at[d], to
            ).start()

    holds(member, finish)

    for copy in cent_sends:
        copy.wait_recv()
    cent_out[head] = cent_in[head, head]
    for k in range(1, heads):
        source = flipped(head, k)
        cent_out[source] = cent_in[heads, k]

    for d in range(1, n):
        source = (me + n - d) % n

        def take(source=source, d=d):
            piece = att.at[(source // 2) % heads, source // (2 * heads) * 2 + source % 2]
            remote(piece, piece, o_send.at[d], o_recv.at[d], source).wait_recv()

        holds(source // (2 * heads) * 2 + source % 2, take)
    per = piece_rows // group
    for s in range(heads):
        for p in range(pieces):
            att_out[p * per : (p + 1) * per, s] = (
                att[s, p].astype(jnp.float32).reshape(per, group, dim).astype(jnp.bfloat16)
            )

    for copy in (
        key_sends + value_sends + first_starts + first_halves + gathers + mass_starts
        + mass_halves + second_starts + second_halves + cent_sends
    ):
        copy.wait_send()
    for d in range(1, members):
        to = (member + d) % members

        def gave(to=to, d=d):
            remote(parts.at[to], fin.at[d], f_send.at[d], f_recv.at[d], at(head, to)).wait_send()

        holds(to, gave)

    def told():
        piece = att.at[head, member]
        for d in range(1, n):
            remote(piece, piece, o_send.at[d], o_recv.at[d], (me + d) % n).wait_send()

    holds(member, told)


def body(
    key_cache,
    value_cache,
    init_centroids,
    block_clusters,
    chosen_clusters,
    request_positions,
    queries,
):
    n = lax.axis_size("ctx")
    heads, tok_dev, dim = key_cache.shape
    requests, _, group, _ = queries.shape
    clusters = init_centroids.shape[1]
    members = n // heads
    chips = members // 2
    share = clusters // members
    owned = clusters // n
    piece_rows = max(group, requests * group // members)
    pieces = requests * group // piece_rows
    f32, bf16 = jnp.float32, jnp.bfloat16
    vmem, dma = pltpu.VMEM, pltpu.SemaphoreType.DMA
    anywhere = pl.BlockSpec(memory_space=pl.ANY)
    in_vmem = pl.BlockSpec(memory_space=pltpu.VMEM)
    in_smem = pl.BlockSpec(memory_space=pltpu.SMEM)
    half = (chips, share, dim)
    tile = math.gcd(256, tok_dev)
    tiles = tok_dev // tile
    return tuple(
        pl.pallas_call(
            functools.partial(kernel, n, tile),
            out_shape=(
                jax.ShapeDtypeStruct((heads, owned, dim), f32),
                jax.ShapeDtypeStruct(queries.shape, bf16),
            ),
            in_specs=[anywhere, anywhere, anywhere, in_vmem, in_vmem, in_smem, in_smem],
            out_specs=(in_vmem, in_vmem),
            scratch_shapes=[
                vmem((clusters, dim), bf16),
                vmem((heads, tok_dev, dim), bf16),
                vmem((heads * tiles, tile, dim), bf16),
                vmem((heads, tok_dev, dim), bf16),
                vmem((members, share, dim), bf16),
                vmem((heads * tiles, members, share, tile), bf16),
                vmem((chips, 2, share, dim), f32),
                vmem((chips, 2, share, dim), f32),
                vmem((chips, 2, share, dim), f32),
                vmem((members, share, BLOCK), f32),
                vmem((chips, 2, 8, share), f32),
                vmem(half, f32),
                vmem(half, bf16),
                vmem(half, bf16),
                vmem(half, f32),
                vmem(half, f32),
                vmem((chips, 8, share), f32),
                vmem(half, bf16),
                vmem(half, bf16),
                vmem((chips, 8, share), f32),
                vmem(half, bf16),
                vmem(half, bf16),
                vmem((chips, 8, share), f32),
                vmem((members, share, dim), bf16),
                vmem((heads + 1, heads, owned, dim), f32),
                vmem((pieces, 3, piece_rows, dim), f32),
                vmem((members, 3, piece_rows, dim), f32),
                vmem((heads, pieces, piece_rows, dim), bf16),
                dma((3,)),
                dma((heads,)),
                dma((heads,)),
                dma((heads,)),
                dma((heads,)),
                dma((4, chips)),
                dma((4, chips)),
                dma((4, chips)),
                dma((4, chips)),
                dma((members,)),
                dma((members,)),
                dma((heads,)),
                dma((heads,)),
                dma((members,)),
                dma((members,)),
                dma((n,)),
                dma((n,)),
            ],
            compiler_params=pltpu.CompilerParams(
                collective_id=0, has_side_effects=True, vmem_limit_bytes=56 * 1024 * 1024
            ),
        )(
            key_cache,
            value_cache,
            init_centroids,
            queries,
            chosen_clusters,
            block_clusters,
            request_positions,
        )
    )


def solution(mesh):
    placed = (
        P(None, ("groups", "ctx"), None),
        P(None, ("groups", "ctx"), None),
        P(),
        P(None, "groups"),
        P("groups", None, None),
        P("groups"),
        P("groups", None, None, None),
    )
    return jax.shard_map(
        body,
        mesh=mesh,
        in_specs=placed,
        out_specs=(P(None, ("groups", "ctx"), None), P("groups", None, None, None)),
        check_vma=False,
    )
```

profile of v0, /device:TPU:0, one launch (start us, length us, event | category | flops | bytes accessed | tf_op | source)
XLA Modules:
  0.0 53.9 jit_solution(17429796680163382363)
XLA Ops:
  0.6 51.0 %shard_map.86 = (f32[4,64,128]{2,1,0:T(8,128)}, bf16[8,4,8,128]{3,2,1,0:T(8,128)(2,1)}) custom-call(bf16[4,512,128]{2,1,0:T(8,128)(2,1)} %key_hbm.1, bf16[4,512,128]{2,1,0:T(8,128)(2,1)} %value_hbm.1, bf16[4,1024,128]{2,1,0:T(8,128)(2,1)} %init_hbm.1, bf16[8,4,8,128]{3,2,1,0:T(8,128)(2,1)} %queries_ref.1, s32[8,4,32]{2,1,0:T(4,128)} %chosen_ref.1, ...), custom_call_target="tpu_custom_call" | custom-call | tf_op jit(solution)/shard_map/pallas_call | solution.py:459
  51.6 0.0 copy-start
  51.6 1.6 %copy.11 = f32[4,64,128]{2,1,0:T(8,128)} copy(f32[4,64,128]{2,1,0:T(8,128)} %get-tuple-element.4) | data formatting | bytes 262144
  53.2 0.0 copy-done
  53.2 0.6 %copy.12 = bf16[8,4,8,128]{3,2,1,0:T(8,128)(2,1)} copy(bf16[8,4,8,128]{3,2,1,0:T(8,128)(2,1)S(1)} %copy-done) | data formatting | bytes 131072
Async XLA Ops:
  51.6 1.6 %copy-start = (bf16[8,4,8,128]{3,2,1,0:T(8,128)(2,1)S(1)}, bf16[8,4,8,128]{3,2,1,0:T(8,128)(2,1)}, u32[]{:S(2)}) copy-start(bf16[8,4,8,128]{3,2,1,0:T(8,128)(2,1)} %get-tuple-element.5) | copy-start | bytes 196612
where the time goes:
time: 54 us; the launch traced here: 53.9 us
  Pallas kernels  51 us (94%)
  local copies, waits for them, and re-layouts  2.23 us (4%)
  between operations  0.65 us (1%)
    pallas_call x1, Pallas kernels, body(): pl.pallas_call(functools.partial(kernel, n, tile), out_shape=(jax.ShapeDt...  51 us
    unnamed x4, local copies, waits for them, and re-layouts  2.23 us

commit v1 on v0

--- a/solution.py
+++ b/solution.py
@@ -42,16 +42,16 @@
 def kernel(
     n,
     tile,
-    key_hbm, value_hbm, init_hbm, queries_ref, chosen_ref, blocks_ref, positions_ref,
+    key_hbm, value_hbm, init_hbm, queries_hbm, chosen_hbm, blocks_hbm, positions_hbm,
     cent_out, att_out,
-    init_v, keys, units, values, cents, held, sums, sums_k, sums_v, mass_acc, mass,
+    queries_ref, chosen_ref, blocks_ref, positions_ref, init_v, keys, units, values, cents, held, sums, sums_k, sums_v, mass_acc, mass,
     first_a, first_half, first_b, keys_a, vals_a, mass_a, keys_half, vals_half, mass_half,
     keys_b, vals_b, mass_b, unit_cents, cent_in, parts, fin, att,
-    local_sem, k_send, k_recv, v_send, v_recv, a_send, a_recv, b_send, b_recv,
+    local_sem, small_sem, k_send, k_recv, v_send, v_recv, a_send, a_recv, b_send, b_recv,
     g_send, g_recv, c_send, c_recv, f_send, f_recv, o_send, o_recv,
 ):
     heads, tok_dev, dim = key_hbm.shape
-    requests, _, group, _ = queries_ref.shape
+    requests, _, group, _ = queries_hbm.shape
     rows = requests * group
     members = n // heads
     chips = members // 2
@@ -70,10 +70,12 @@
 
 
     barrier = pltpu.get_barrier_semaphore()
-    for step in range(1, n):
-        pl.semaphore_signal(
-            barrier, inc=1, device_id={"ctx": (me + step) % n}, device_id_type=MESH
-        )
+    partner = me + 1 - 2 * core
+    peers = [partner]
+    peers += [at(flipped(head, k), member) for k in range(1, heads)]
+    peers += [at(head, (chip + d) % chips * 2 + core) for d in range(1, chips)]
+    for peer in peers:
+        pl.semaphore_signal(barrier, inc=1, device_id={"ctx": peer}, device_id_type=MESH)
 
     def remote(src, dst, send, recv, target):
         return pltpu.make_async_remote_copy(
@@ -87,7 +89,17 @@
     init_copy.start()
     key_copy.start()
     value_copy.start()
-    pl.semaphore_wait(barrier, n - 1)
+    small = (
+        (queries_hbm, queries_ref), (chosen_hbm, chosen_ref),
+        (blocks_hbm, blocks_ref), (positions_hbm, positions_ref),
+    )
+    small_copies = [
+        pltpu.make_async_copy(source, here, small_sem.at[index])
+        for index, (source, here) in enumerate(small)
+    ]
+    for copy in small_copies:
+        copy.start()
+    pl.semaphore_wait(barrier, len(peers))
 
     key_sends, value_sends = [], []
     for k in range(1, heads):
@@ -151,8 +163,6 @@
             own = own + slots[d].astype(jnp.float32)
         return own
 
-    partner = me + 1 - 2 * core
-
     key_copy.wait()
     for k in range(heads):
         if k:
@@ -198,6 +208,8 @@
         share_out(member, d, at(head, (chip + d) % chips * 2 + core))
     share_out(member, chips, partner)
 
+    for copy in small_copies:
+        copy.wait()
     row_ids = lax.broadcasted_iota(jnp.int32, (rows, 1), 0)
     seen = jnp.zeros((rows, 1), jnp.int32)
     for r in range(requests):
@@ -426,6 +438,17 @@
             remote(piece, piece, o_send.at[d], o_recv.at[d], (me + d) % n).wait_send()
 
     holds(member, told)
+
+
+def put_out(cent_in, att_in, cent_out, att_out, sem):
+    copies = (
+        pltpu.make_async_copy(cent_in, cent_out, sem.at[0]),
+        pltpu.make_async_copy(att_in, att_out, sem.at[1]),
+    )
+    for copy in copies:
+        copy.start()
+    for copy in copies:
+        copy.wait()
 
 
 def body(
@@ -451,20 +474,23 @@
     vmem, dma = pltpu.VMEM, pltpu.SemaphoreType.DMA
     anywhere = pl.BlockSpec(memory_space=pl.ANY)
     in_vmem = pl.BlockSpec(memory_space=pltpu.VMEM)
-    in_smem = pl.BlockSpec(memory_space=pltpu.SMEM)
     half = (chips, share, dim)
     tile = math.gcd(256, tok_dev)
     tiles = tok_dev // tile
-    return tuple(
+    results = (
         pl.pallas_call(
             functools.partial(kernel, n, tile),
             out_shape=(
-                jax.ShapeDtypeStruct((heads, owned, dim), f32),
-                jax.ShapeDtypeStruct(queries.shape, bf16),
+                vmem((heads, owned, dim), f32),
+                vmem(queries.shape, bf16),
             ),
-            in_specs=[anywhere, anywhere, anywhere, in_vmem, in_vmem, in_smem, in_smem],
+            in_specs=[anywhere] * 7,
             out_specs=(in_vmem, in_vmem),
             scratch_shapes=[
+                vmem(queries.shape, bf16),
+                vmem(chosen_clusters.shape, jnp.int32),
+                pltpu.SMEM(block_clusters.shape, jnp.int32),
+                pltpu.SMEM(request_positions.shape, jnp.int32),
                 vmem((clusters, dim), bf16),
                 vmem((heads, tok_dev, dim), bf16),
                 vmem((heads * tiles, tile, dim), bf16),
@@ -494,6 +520,7 @@
                 vmem((members, 3, piece_rows, dim), f32),
                 vmem((heads, pieces, piece_rows, dim), bf16),
                 dma((3,)),
+                dma((4,)),
                 dma((heads,)),
                 dma((heads,)),
                 dma((heads,)),
@@ -524,6 +551,15 @@
             request_positions,
         )
     )
+    return tuple(
+        pl.pallas_call(
+            put_out,
+            out_shape=tuple(jax.ShapeDtypeStruct(x.shape, x.dtype) for x in results),
+            in_specs=[anywhere, anywhere],
+            out_specs=(anywhere, anywhere),
+            scratch_shapes=[dma((2,))],
+        )(*(pltpu.with_memory_space_constraint(x, pltpu.VMEM) for x in results))
+    )
 
 
 def solution(mesh):

time: 54 us -> 50.1 us (0.928)
  local copies, waits for them, and re-layouts: 2.23 us -> 0 us
  Pallas kernels: 51 us -> 49.3 us
    unnamed x4 -> x0, local copies, waits for them, and re-layouts: 2.23 us -> none
    pallas_call x1 -> x2, Pallas kernels: 51 us -> 49.3 us  [the longest x1 48.7 us: body(): pl.pallas_call(functools.partial(kernel, n, tile), out_shape=(vmem((heads...]
where the time goes in v1:
time: 50.1 us; the launch traced here: 50 us
  Pallas kernels  49.3 us (98%)
  between operations  0.64 us (1%)
    pallas_call x1, Pallas kernels, body(): pl.pallas_call(functools.partial(kernel, n, tile), out_shape=(vmem((heads...  48.7 us

profile of v1, /device:TPU:0, one launch (start us, length us, event | category | flops | bytes accessed | tf_op | source)
XLA Modules:
  0.0 50.0 jit_solution(13765240529316577633)
XLA Ops:
  0.6 48.7 %shard_map.86 = (f32[4,64,128]{2,1,0:T(8,128)S(1)}, bf16[8,4,8,128]{3,2,1,0:T(8,128)(2,1)S(1)}) custom-call(bf16[4,512,128]{2,1,0:T(8,128)(2,1)} %key_hbm.1, bf16[4,512,128]{2,1,0:T(8,128)(2,1)} %value_hbm.1, bf16[4,1024,128]{2,1,0:T(8,128)(2,1)} %init_hbm.1, bf16[8,4,8,128]{3,2,1,0:T(8,128)(2,1)} %queries_hbm.1, s32[8,4,32]{2,1,0:T(4,128)} %chosen_hbm.1, ...), custom_call_target="tpu_custom_call" | custom-call | tf_op jit(solution)/shard_map/pallas_call | solution.py:481
  49.3 0.7 %shard_map.87 = (f32[4,64,128]{2,1,0:T(8,128)}, bf16[8,4,8,128]{3,2,1,0:T(8,128)(2,1)}) custom-call(f32[4,64,128]{2,1,0:T(8,128)S(1)} %get-tuple-element.4.cent_in, bf16[8,4,8,128]{3,2,1,0:T(8,128)(2,1)S(1)} %get-tuple-element.5.att_in), custom_call_target="tpu_custom_call" | custom-call | tf_op jit(solution)/shard_map/pallas_call | solution.py:555

commit v2 on v1

v2 whole, which is shorter than its diff:
```python
import functools
import math

import jax
import jax.numpy as jnp
from jax import lax
from jax.experimental import pallas as pl
from jax.experimental.pallas import tpu as pltpu
from jax.sharding import PartitionSpec as P

BLOCK = 128
SHARPNESS = 16.0
EPSILON = 1e-06
NEGATIVE = -1e30
MESH = pl.DeviceIdType.MESH
NT = (((1,), (1,)), ((), ()))
NN = (((1,), (0,)), ((), ()))


def to_unit(vectors):
    vectors = vectors.astype(jnp.float32)
    return (
        vectors
        * lax.rsqrt(jnp.mean(vectors * vectors, axis=-1, keepdims=True) + EPSILON)
        * vectors.shape[-1] ** (-0.5)
    )


def flipped(index, bits):
    bit = 1
    while bit <= bits:
        if bits & bit:
            index = index + bit * (1 - 2 * ((index // bit) % 2))
        bit *= 2
    return index


def dot(a, b, dims, precision=None):
    return lax.dot_general(a, b, dims, preferred_element_type=jnp.float32, precision=precision)


def kernel(
    n,
    tile,
    key_hbm, value_hbm, init_hbm, queries_hbm, chosen_hbm, blocks_hbm, positions_hbm,
    cent_out, att_out,
    queries_ref, chosen_ref, blocks_ref, positions_ref, init_v, keys, units, values, cents, held,
    scaled, den, invs, sums, sums_k, sums_v, mass,
    first_a, first_half, first_b, keys_a, vals_a, mass_a, keys_half, vals_half, mass_half,
    keys_b, vals_b, mass_b, unit_cents, cent_in, parts, fin, att,
    local_sem, small_sem, k_send, k_recv, v_send, v_recv, a_send, a_recv, b_send, b_recv,
    g_send, g_recv, c_send, c_recv, f_send, f_recv, o_send, o_recv,
):
    heads, tok_dev, dim = key_hbm.shape
    requests, _, group, _ = queries_hbm.shape
    rows = requests * group
    members = n // heads
    chips = members // 2
    cuts, crow = first_a.shape[1], first_a.shape[2]
    share = cuts * crow
    owned = share // heads
    tiles = tok_dev // tile
    pieces, piece_rows = att.shape[1], att.shape[2]
    me = lax.axis_index("ctx")
    head, core, chip = (me // 2) % heads, me % 2, me // (2 * heads)
    member = chip * 2 + core
    other = 1 - core

    def at(of_head, of_member):
        return (of_member // 2) * (2 * heads) + of_head * 2 + of_member % 2

    barrier = pltpu.get_barrier_semaphore()
    partner = me + 1 - 2 * core
    peers = [partner]
    peers += [at(flipped(head, k), member) for k in range(1, heads)]
    peers += [at(head, (chip + d) % chips * 2 + core) for d in range(1, chips)]
    for peer in peers:
        pl.semaphore_signal(barrier, inc=1, device_id={"ctx": peer}, device_id_type=MESH)

    sent = []

    def remote(src, dst, send, recv, target):
        return pltpu.make_async_remote_copy(
            src_ref=src, dst_ref=dst, send_sem=send, recv_sem=recv,
            device_id={"ctx": target}, device_id_type=MESH,
        )

    def begin(*args):
        copy = remote(*args)
        copy.start()
        sent.append(copy)
        return copy

    init_copy = pltpu.make_async_copy(init_hbm.at[head], init_v, local_sem.at[0])
    key_copy = pltpu.make_async_copy(key_hbm.at[head], keys.at[0], local_sem.at[1])
    value_copy = pltpu.make_async_copy(value_hbm.at[head], values.at[0], local_sem.at[2])
    init_copy.start()
    key_copy.start()
    value_copy.start()
    small = (
        (queries_hbm, queries_ref), (chosen_hbm, chosen_ref),
        (blocks_hbm, blocks_ref), (positions_hbm, positions_ref),
    )
    small_copies = [
        pltpu.make_async_copy(source, here, small_sem.at[index])
        for index, (source, here) in enumerate(small)
    ]
    for copy in small_copies:
        copy.start()
    pl.semaphore_wait(barrier, len(peers))

    key_sends, value_sends = {}, []
    for k in range(1, heads):
        to = flipped(head, k)
        for j in range(tiles):
            span = pl.ds(j * tile, tile)
            key_sends[k, j] = begin(
                key_hbm.at[to, span], keys.at[k, span], k_send.at[k, j], k_recv.at[k, j],
                at(to, member),
            )

    def send_values(k):
        to = flipped(head, k)
        value_sends.append(
            begin(value_hbm.at[to], values.at[k], v_send.at[k], v_recv.at[k], at(to, member))
        )

    if heads > 1:
        send_values(1)

    init_copy.wait()
    start = to_unit(init_v[...]).reshape(chips, heads, 2, owned, dim)
    for part in range(members):
        rows_of = jnp.concatenate(
            [start[part // 2, s, part % 2] for s in range(heads)], axis=0
        ).astype(jnp.bfloat16)
        for c in range(cuts):
            cents[part * cuts + c] = rows_of[c * crow : (c + 1) * crow]

    def raised_of(current, unit_keys):
        cosine = dot(current, unit_keys, NT)
        return jnp.exp2(cosine * (SHARPNESS * math.log2(math.e)))

    def folded(raised):
        return jnp.sum(raised.reshape(raised.shape[0] // 8, 8, raised.shape[1]), axis=0)

    def inverse(folds):
        return 1.0 / jnp.sum(folds, axis=0, keepdims=True)

    def column(row):
        return jnp.broadcast_to(row, (dim, row.shape[1])).T

    per = max(1, min(members * cuts, 128 // crow))

    def span_of(t):
        return slice(t * tile, (t + 1) * tile)

    def block_of(k):
        return slice(k * tok_dev, (k + 1) * tok_dev)

    key_copy.wait()
    for k in range(heads):
        for j in range(tiles):
            t = k * tiles + j
            if k:
                key_sends[k, j].wait_recv()
            own_keys = keys[k, span_of(j)].astype(jnp.float32)
            unit = to_unit(own_keys).astype(jnp.bfloat16)
            units[t] = unit
            folds = None
            for g in range(0, members * cuts, per):
                raised = raised_of(cents[g : g + per].reshape(per * crow, dim), unit)
                held[g : g + per, :, span_of(t)] = raised.astype(jnp.bfloat16).reshape(
                    per, crow, tile
                )
                folds = folded(raised) if folds is None else folds + folded(raised)
            scaled[span_of(t), :dim] = (own_keys * column(inverse(folds))).astype(jnp.bfloat16)
        if k < heads - 1:
            for index in range(members * cuts):
                term = dot(held[index, :, block_of(k)], scaled[block_of(k), :dim], NN)
                sums[index] = term if k == 0 else sums[index] + term

    def first_part(place, side, c):
        index = (place * 2 + side) * cuts + c
        last = block_of(heads - 1)
        return sums[index] + dot(held[index, :, last], scaled[last, :dim], NN)

    first_own = []
    for d in range(chips):
        place = (chip + d + 1) % chips
        arrivals = []
        for c in range(cuts):
            index = (place * 2 + other) * cuts + c
            sums[index] = first_part(place, other, c)
            arrivals.append(
                begin(
                    sums.at[index], first_a.at[d, c], a_send.at[0, d, c], a_recv.at[0, d, c],
                    partner,
                )
            )
        for c in range(cuts):
            term = first_part(place, core, c)
            arrivals[c].wait_recv()
            term = term + first_a[d, c]
            if d == chips - 1:
                first_own.append(term)
                continue
            first_half[d, c] = term.astype(first_half.dtype)
            begin(
                first_half.at[d, c], first_b.at[d, c], b_send.at[0, d, c], b_recv.at[0, d, c],
                at(head, place * 2 + core),
            )

    for k in range(2, min(3, heads)):
        send_values(k)

    for copy in small_copies:
        copy.wait()
    row_ids = lax.broadcasted_iota(jnp.int32, (rows, 1), 0)
    seen = jnp.zeros((rows, 1), jnp.int32)
    for r in range(requests):
        seen = jnp.where(row_ids // group == r, positions_ref[r], seen)
    chosen = chosen_ref[:, 0, :]
    for s in range(1, heads):
        chosen = jnp.where(head == s, chosen_ref[:, s, :], chosen)
    ksel = chosen.shape[1]
    chosen = jnp.broadcast_to(chosen[:, None, :], (requests, group, ksel)).reshape(rows, ksel)
    query = queries_ref[:, head].astype(jnp.float32).reshape(rows, dim).astype(jnp.bfloat16)
    scale = dim ** (-0.5)
    lanes = lax.broadcasted_iota(jnp.int32, (rows, BLOCK), 1)

    def exact_scores():
        found = []
        for k in range(heads):
            device = at(flipped(head, k), member)
            score = dot(query, keys[k], NT) * scale
            for b in range(tok_dev // BLOCK):
                cluster = blocks_ref[head, device * (tok_dev // BLOCK) + b]
                hits = jnp.max(jnp.where(chosen == cluster, 1, 0), axis=1, keepdims=True) > 0
                place = device * tok_dev + b * BLOCK + lanes
                usable = hits & (place < seen)
                found.append(
                    jnp.where(usable, score[:, b * BLOCK : (b + 1) * BLOCK], NEGATIVE)
                )
        return jnp.concatenate(found, axis=1)

    exact = exact_scores()
    exact_peak = jnp.max(exact, axis=1, keepdims=True)
    exact_prob = jnp.where(exact > 0.5 * NEGATIVE, jnp.exp(exact - exact_peak), 0.0).astype(
        jnp.bfloat16
    )
    exact_sum = jnp.sum(exact_prob.astype(jnp.float32), axis=1, keepdims=True)
    lane_ids = lax.broadcasted_iota(jnp.int32, (rows, share), 1)
    cluster_ids = at(lane_ids // owned, member) * owned + lane_ids % owned
    picked = chosen[:, 0:1] == cluster_ids
    for k in range(1, ksel):
        picked = picked | (chosen[:, k : k + 1] == cluster_ids)
    picked = jnp.where(picked, 1.0, 0.0)

    den[...] = jnp.zeros_like(den)

    def weigh(index):
        for t in range(heads * tiles):
            raised = raised_of(unit_cents[index], units[t])
            held[index, :, span_of(t)] = raised.astype(jnp.bfloat16)
            den[t] += folded(raised)

    def gathered(place, slot, c):
        index = place * cuts + c
        piece = unit_cents.at[index]
        remote(piece, piece, g_send.at[slot, c], g_recv.at[slot, c], partner).wait_recv()
        return index

    def share_out(index, slot, c, target):
        piece = unit_cents.at[index]
        begin(piece, piece, g_send.at[slot, c], g_recv.at[slot, c], target)

    for c in range(cuts):
        own = first_own[c]
        for d in range(chips - 1):
            slot = first_b.at[d, c]
            remote(
                slot, slot, b_send.at[0, d, c], b_recv.at[0, d, c], partner
            ).wait_recv()
            own = own + first_b[d, c].astype(jnp.float32)
        index = member * cuts + c
        unit_cents[index] = to_unit(own).astype(jnp.bfloat16)
        for d in range(1, chips):
            share_out(index, d, c, at(head, (chip + d) % chips * 2 + core))
        share_out(index, chips, c, partner)
        if c == cuts - 1:
            for k in range(3, heads):
                send_values(k)
        weigh(index)
        weigh(gathered(chip * 2 + other, chips, c))
    for d in range(1, chips):
        place = (chip + chips - d) % chips * 2
        for c in range(cuts):
            index = gathered(place + core, d, c)
            share_out(index, chips + d, c, partner)
            weigh(index)
    for d in range(1, chips):
        place = (chip + chips - d) % chips * 2
        for c in range(cuts):
            weigh(gathered(place + other, chips + d, c))

    value_copy.wait()
    for copy in value_sends:
        copy.wait_recv()
    term_ids = lax.broadcasted_iota(jnp.int32, (invs.shape[1], tile), 0)
    for t in range(heads * tiles):
        k, j = t // tiles, t % tiles
        inv = inverse(den[t])
        high = inv.astype(jnp.bfloat16).astype(jnp.float32)
        invs[t] = jnp.where(
            term_ids == 0, high, jnp.where(term_ids == 1, inv - high, 0.0)
        ).astype(jnp.bfloat16)
        wide = column(inv)
        for side, source in enumerate((keys, values)):
            scaled[span_of(t), side * dim : (side + 1) * dim] = (
                source[k, span_of(j)].astype(jnp.float32) * wide
            ).astype(jnp.bfloat16)

    def second_part(place, side, c):
        total = dot(held[(place * 2 + side) * cuts + c], scaled[...], NN)
        return total[:, :dim], total[:, dim:]

    def mass_part(place, side, c):
        index = (place * 2 + side) * cuts + c
        total = None
        for t in range(heads * tiles):
            term = dot(invs[t], held[index, :, span_of(t)], NT)
            total = term if total is None else total + term
        return jnp.broadcast_to(total[0:1] + total[1:2], (8, crow))

    flows = ((sums_k, keys_a, keys_half, keys_b), (sums_v, vals_a, vals_half, vals_b))
    own_sums = [[None] * cuts, [None] * cuts]
    own_masses = None
    for d in range(chips):
        place = (chip + d + 1) % chips
        far = at(head, place * 2 + core)
        arrivals = {}
        for c in range(cuts):
            index = (place * 2 + other) * cuts + c
            for flow, (term, (mine, came, _, _)) in enumerate(
                zip(second_part(place, other, c), flows)
            ):
                mine[index] = term
                arrivals[flow, c] = begin(
                    mine.at[index], came.at[d, c], a_send.at[1 + flow, d, c],
                    a_recv.at[1 + flow, d, c], partner,
                )
        for c in range(cuts):
            mass[place, c] = mass_part(place, other, c)
        mass_arrival = begin(
            mass.at[place], mass_a.at[d], a_send.at[3, d, 0], a_recv.at[3, d, 0], partner
        )
        for c in range(cuts):
            terms = second_part(place, core, c)
            if c == cuts - 1:
                masses = [mass_part(place, core, e) for e in range(cuts)]
                mass_arrival.wait_recv()
                masses = [masses[e] + mass_a[d, e] for e in range(cuts)]
                if d == chips - 1:
                    own_masses = masses
                else:
                    for e in range(cuts):
                        mass_half[d, e] = masses[e]
                    begin(
                        mass_half.at[d], mass_b.at[d], b_send.at[3, d, 0], b_recv.at[3, d, 0], far
                    )
            for flow, (term, (_, came, half, slots)) in enumerate(zip(terms, flows)):
                arrivals[flow, c].wait_recv()
                term = term + came[d, c]
                if d == chips - 1:
                    own_sums[flow][c] = term
                    continue
                half[d, c] = term.astype(half.dtype)
                begin(
                    half.at[d, c], slots.at[d, c], b_send.at[1 + flow, d, c],
                    b_recv.at[1 + flow, d, c], far,
                )

    exact_weighted = dot(exact_prob, values[...].reshape(heads * tok_dev, dim), NN)

    def landed(slots, row, d, c):
        slot = slots.at[d, c]
        remote(slot, slot, b_send.at[row, d, c], b_recv.at[row, d, c], partner).wait_recv()

    for d in range(chips - 1):
        slot = mass_b.at[d]
        remote(slot, slot, b_send.at[3, d, 0], b_recv.at[3, d, 0], partner).wait_recv()
        own_masses = [own_masses[c] + mass_b[d, c] for c in range(cuts)]
    mass_row = jnp.concatenate([m[0:1] for m in own_masses], axis=1)
    log_mass = jnp.log(mass_row)
    eye = lax.broadcasted_iota(jnp.int32, (share, share), 0) == lax.broadcasted_iota(
        jnp.int32, (share, share), 1
    )
    mass_column = jnp.sum(jnp.where(eye, mass_row, 0.0), axis=1, keepdims=True)

    for c in range(cuts):
        for d in range(chips - 1):
            landed(keys_b, 1, d, c)
            own_sums[0][c] = own_sums[0][c] + keys_b[d, c].astype(jnp.float32)
    own_keys = jnp.concatenate(own_sums[0], axis=0)
    cent_in[head] = to_unit(own_keys).reshape(heads, owned, dim)
    cent_sends = []
    for k in range(1, heads):
        to = flipped(head, k)
        cent_sends.append(
            begin(
                cent_in.at[head, to], cent_in.at[heads, k], c_send.at[k], c_recv.at[k],
                at(to, member),
            )
        )

    mean_keys = (own_keys / mass_column).astype(jnp.bfloat16)
    score = dot(query, mean_keys, NT) * scale + log_mass
    usable = picked < 0.5
    score = jnp.where(usable, score, NEGATIVE)
    peak = jnp.maximum(jnp.max(score, axis=1, keepdims=True), exact_peak)
    prob = jnp.where(usable, jnp.exp(score - peak), 0.0).astype(jnp.bfloat16)
    exact_factor = jnp.exp(exact_peak - peak)
    weight_sum = jnp.sum(prob.astype(jnp.float32), axis=1, keepdims=True) + exact_sum * exact_factor
    shape = (pieces, piece_rows, dim)
    stat_lanes = lax.broadcasted_iota(jnp.int32, (rows, dim), 1)
    parts[:, 1] = jnp.where(stat_lanes < dim // 2, weight_sum, peak).reshape(shape)
    for c in range(cuts):
        for d in range(chips - 1):
            landed(vals_b, 2, d, c)
            own_sums[1][c] = own_sums[1][c] + vals_b[d, c].astype(jnp.float32)
    own_values = jnp.concatenate(own_sums[1], axis=0)
    mean_values = (own_values / mass_column).astype(jnp.bfloat16)
    weighted = dot(prob, mean_values, NN) + exact_weighted * exact_factor
    parts[:, 0] = weighted.reshape(shape)

    def holds(index, action):
        if pieces == members:
            action()
        else:
            pl.when(index < pieces)(action)

    for d in range(1, members):
        to = (member + d) % members

        def give(to=to, d=d):
            remote(parts.at[to], fin.at[d], f_send.at[d], f_recv.at[d], at(head, to)).start()

        holds(to, give)

    def finish():
        for d in range(1, members):
            remote(parts.at[0], fin.at[d], f_send.at[d], f_recv.at[d], partner).wait_recv()
        stats = [parts[member]] + [fin[d] for d in range(1, members)]
        peaks = [stat[1][:, dim - 1 :] for stat in stats]
        top = functools.reduce(jnp.maximum, peaks)
        upper, lower = 0.0, 0.0
        for stat, high in zip(stats, peaks):
            factor = jnp.exp(high - top)
            upper = upper + stat[0] * factor
            lower = lower + stat[1][:, :1] * factor
        att[head, member] = (upper / lower).astype(jnp.bfloat16)
        for d in range(1, n):
            to = (me + d) % n
            remote(
                att.at[head, member], att.at[head, member], o_send.at[d], o_recv.at[d], to
            ).start()

    holds(member, finish)

    for copy in cent_sends:
        copy.wait_recv()
    cent_out[head] = cent_in[head, head]
    for k in range(1, heads):
        source = flipped(head, k)
        cent_out[source] = cent_in[heads, k]

    for copy in sent:
        copy.wait_send()
    for d in range(1, members):
        to = (member + d) % members

        def gave(to=to, d=d):
            remote(parts.at[to], fin.at[d], f_send.at[d], f_recv.at[d], at(head, to)).wait_send()

        holds(to, gave)

    for d in range(1, n):
        source = (me + n - d) % n

        def take(source=source, d=d):
            piece = att.at[(source // 2) % heads, source // (2 * heads) * 2 + source % 2]
            remote(piece, piece, o_send.at[d], o_recv.at[d], source).wait_recv()

        holds(source // (2 * heads) * 2 + source % 2, take)
    per_piece = piece_rows // group
    for s in range(heads):
        for p in range(pieces):
            att_out[p * per_piece : (p + 1) * per_piece, s] = (
                att[s, p].astype(jnp.float32).reshape(per_piece, group, dim).astype(jnp.bfloat16)
            )

    def told():
        piece = att.at[head, member]
        for d in range(1, n):
            remote(piece, piece, o_send.at[d], o_recv.at[d], (me + d) % n).wait_send()

    holds(member, told)


def put_out(cent_in, att_in, cent_out, att_out, sem):
    copies = (
        pltpu.make_async_copy(cent_in, cent_out, sem.at[0]),
        pltpu.make_async_copy(att_in, att_out, sem.at[1]),
    )
    for copy in copies:
        copy.start()
    for copy in copies:
        copy.wait()


def body(
    key_cache,
    value_cache,
    init_centroids,
    block_clusters,
    chosen_clusters,
    request_positions,
    queries,
):
    n = lax.axis_size("ctx")
    heads, tok_dev, dim = key_cache.shape
    requests, _, group, _ = queries.shape
    clusters = init_centroids.shape[1]
    members = n // heads
    chips = members // 2
    share = clusters // members
    owned = clusters // n
    cuts = 2 if share % 256 == 0 else 1
    crow = share // cuts
    piece_rows = max(group, requests * group // members)
    pieces = requests * group // piece_rows
    f32, bf16 = jnp.float32, jnp.bfloat16
    vmem, dma = pltpu.VMEM, pltpu.SemaphoreType.DMA
    anywhere = pl.BlockSpec(memory_space=pl.ANY)
    in_vmem = pl.BlockSpec(memory_space=pltpu.VMEM)
    whole = (members * cuts, crow, dim)
    half = (chips, cuts, crow, dim)
    small = (chips, cuts, 8, crow)
    tile = math.gcd(256, tok_dev)
    tiles = tok_dev // tile
    tokens = heads * tok_dev
    results = pl.pallas_call(
        functools.partial(kernel, n, tile),
        out_shape=(
            vmem((heads, owned, dim), f32),
            vmem(queries.shape, bf16),
        ),
        in_specs=[anywhere] * 7,
        out_specs=(in_vmem, in_vmem),
        scratch_shapes=[
            vmem(queries.shape, bf16),
            vmem(chosen_clusters.shape, jnp.int32),
            pltpu.SMEM(block_clusters.shape, jnp.int32),
            pltpu.SMEM(request_positions.shape, jnp.int32),
            vmem((clusters, dim), bf16),
            vmem((heads, tok_dev, dim), bf16),
            vmem((heads * tiles, tile, dim), bf16),
            vmem((heads, tok_dev, dim), bf16),
            vmem(whole, bf16),
            vmem((members * cuts, crow, tokens), bf16),
            vmem((tokens, 2 * dim), bf16),
            vmem((heads * tiles, 8, tile), f32),
            vmem((heads * tiles, 16, tile), bf16),
            vmem(whole, f32),
            vmem(whole, f32),
            vmem(whole, f32),
            vmem(small, f32),
            vmem(half, f32),
            vmem(half, bf16),
            vmem(half, bf16),
            vmem(half, f32),
            vmem(half, f32),
            vmem(small, f32),
            vmem(half, bf16),
            vmem(half, bf16),
            vmem(small, f32),
            vmem(half, bf16),
            vmem(half, bf16),
            vmem(small, f32),
            vmem(whole, bf16),
            vmem((heads + 1, heads, owned, dim), f32),
            vmem((pieces, 2, piece_rows, dim), f32),
            vmem((members, 2, piece_rows, dim), f32),
            vmem((heads, pieces, piece_rows, dim), bf16),
            dma((3,)),
            dma((4,)),
            dma((heads, tiles)),
            dma((heads, tiles)),
            dma((heads,)),
            dma((heads,)),
            dma((4, chips, cuts)),
            dma((4, chips, cuts)),
            dma((4, chips, cuts)),
            dma((4, chips, cuts)),
            dma((2 * chips, cuts)),
            dma((2 * chips, cuts)),
            dma((heads,)),
            dma((heads,)),
            dma((members,)),
            dma((members,)),
            dma((n,)),
            dma((n,)),
        ],
        compiler_params=pltpu.CompilerParams(
            collective_id=0, has_side_effects=True, vmem_limit_bytes=56 * 1024 * 1024
        ),
    )(
        key_cache,
        value_cache,
        init_centroids,
        queries,
        chosen_clusters,
        block_clusters,
        request_positions,
    )
    return tuple(
        pl.pallas_call(
            put_out,
            out_shape=tuple(jax.ShapeDtypeStruct(x.shape, x.dtype) for x in results),
            in_specs=[anywhere, anywhere],
            out_specs=(anywhere, anywhere),
            scratch_shapes=[dma((2,))],
        )(*(pltpu.with_memory_space_constraint(x, pltpu.VMEM) for x in results))
    )


def solution(mesh):
    placed = (
        P(None, ("groups", "ctx"), None),
        P(None, ("groups", "ctx"), None),
        P(),
        P(None, "groups"),
        P("groups", None, None),
        P("groups"),
        P("groups", None, None, None),
    )
    return jax.shard_map(
        body,
        mesh=mesh,
        in_specs=placed,
        out_specs=(P(None, ("groups", "ctx"), None), P("groups", None, None, None)),
        check_vma=False,
    )
```

time: 50.1 us -> 50.7 us (1.012)
  Pallas kernels: 49.3 us -> 49.9 us
    pallas_call x1, Pallas kernels: 48.7 us -> 49.2 us  [body(): pl.pallas_call(functools.partial(kernel, n, tile), out_shape=(vmem((heads...]
where the time goes in v2:
time: 50.7 us; the launch traced here: 50.5 us
  Pallas kernels  49.9 us (98%)
  between operations  0.64 us (1%)
    pallas_call x1, Pallas kernels, body(): pl.pallas_call(functools.partial(kernel, n, tile), out_shape=(vmem((heads...  49.2 us

profile of v2, /device:TPU:0, one launch (start us, length us, event | category | flops | bytes accessed | tf_op | source)
XLA Modules:
  0.0 50.5 jit_solution(833616169584731407)
XLA Ops:
  0.6 49.2 %shard_map.86 = (f32[4,64,128]{2,1,0:T(8,128)S(1)}, bf16[8,4,8,128]{3,2,1,0:T(8,128)(2,1)S(1)}) custom-call(bf16[4,512,128]{2,1,0:T(8,128)(2,1)} %key_hbm.1, bf16[4,512,128]{2,1,0:T(8,128)(2,1)} %value_hbm.1, bf16[4,1024,128]{2,1,0:T(8,128)(2,1)} %init_hbm.1, bf16[8,4,8,128]{3,2,1,0:T(8,128)(2,1)} %queries_hbm.1, s32[8,4,32]{2,1,0:T(4,128)} %chosen_hbm.1, ...), custom_call_target="tpu_custom_call" | custom-call | tf_op jit(solution)/shard_map/pallas_call | solution.py:553
  49.8 0.7 %shard_map.87 = (f32[4,64,128]{2,1,0:T(8,128)}, bf16[8,4,8,128]{3,2,1,0:T(8,128)(2,1)}) custom-call(f32[4,64,128]{2,1,0:T(8,128)S(1)} %get-tuple-element.4.cent_in, bf16[8,4,8,128]{3,2,1,0:T(8,128)(2,1)S(1)} %get-tuple-element.5.att_in), custom_call_target="tpu_custom_call" | custom-call | tf_op jit(solution)/shard_map/pallas_call | solution.py:628

commit v3 on v2

--- a/solution.py
+++ b/solution.py
@@ -125,9 +125,6 @@
             begin(value_hbm.at[to], values.at[k], v_send.at[k], v_recv.at[k], at(to, member))
         )
 
-    if heads > 1:
-        send_values(1)
-
     init_copy.wait()
     start = to_unit(init_v[...]).reshape(chips, heads, 2, owned, dim)
     for part in range(members):
@@ -175,10 +172,15 @@
                 )
                 folds = folded(raised) if folds is None else folds + folded(raised)
             scaled[span_of(t), :dim] = (own_keys * column(inverse(folds))).astype(jnp.bfloat16)
+        if k == 1 and heads > 2:
+            send_values(2)
         if k < heads - 1:
             for index in range(members * cuts):
                 term = dot(held[index, :, block_of(k)], scaled[block_of(k), :dim], NN)
                 sums[index] = term if k == 0 else sums[index] + term
+
+    if heads > 1:
+        send_values(1)
 
     def first_part(place, side, c):
         index = (place * 2 + side) * cuts + c
@@ -211,7 +213,7 @@
                 at(head, place * 2 + core),
             )
 
-    for k in range(2, min(3, heads)):
+    for k in range(3, heads):
         send_values(k)
 
     for copy in small_copies:
@@ -288,9 +290,6 @@
         for d in range(1, chips):
             share_out(index, d, c, at(head, (chip + d) % chips * 2 + core))
         share_out(index, chips, c, partner)
-        if c == cuts - 1:
-            for k in range(3, heads):
-                send_values(k)
         weigh(index)
         weigh(gathered(chip * 2 + other, chips, c))
     for d in range(1, chips):

time: 50.7 us -> 45.9 us (0.905)
  Pallas kernels: 49.9 us -> 45.1 us
    pallas_call x1, Pallas kernels: 49.2 us -> 44.4 us  [body(): pl.pallas_call(functools.partial(kernel, n, tile), out_shape=(vmem((heads...]
where the time goes in v3:
time: 45.9 us; the launch traced here: 45.7 us
  Pallas kernels  45.1 us (98%)
  between operations  0.64 us (1%)
    pallas_call x1, Pallas kernels, body(): pl.pallas_call(functools.partial(kernel, n, tile), out_shape=(vmem((heads...  44.4 us

profile of v3, /device:TPU:0, one launch (start us, length us, event | category | flops | bytes accessed | tf_op | source)
XLA Modules:
  0.0 45.7 jit_solution(6002232310506717808)
XLA Ops:
  0.6 44.4 %shard_map.86 = (f32[4,64,128]{2,1,0:T(8,128)S(1)}, bf16[8,4,8,128]{3,2,1,0:T(8,128)(2,1)S(1)}) custom-call(bf16[4,512,128]{2,1,0:T(8,128)(2,1)} %key_hbm.1, bf16[4,512,128]{2,1,0:T(8,128)(2,1)} %value_hbm.1, bf16[4,1024,128]{2,1,0:T(8,128)(2,1)} %init_hbm.1, bf16[8,4,8,128]{3,2,1,0:T(8,128)(2,1)} %queries_hbm.1, s32[8,4,32]{2,1,0:T(4,128)} %chosen_hbm.1, ...), custom_call_target="tpu_custom_call" | custom-call | tf_op jit(solution)/shard_map/pallas_call | solution.py:552
  45.0 0.7 %shard_map.87 = (f32[4,64,128]{2,1,0:T(8,128)}, bf16[8,4,8,128]{3,2,1,0:T(8,128)(2,1)}) custom-call(f32[4,64,128]{2,1,0:T(8,128)S(1)} %get-tuple-element.4.cent_in, bf16[8,4,8,128]{3,2,1,0:T(8,128)(2,1)S(1)} %get-tuple-element.5.att_in), custom_call_target="tpu_custom_call" | custom-call | tf_op jit(solution)/shard_map/pallas_call | solution.py:627

commit v4 on v3

--- a/solution.py
+++ b/solution.py
@@ -47,9 +47,9 @@
     queries_ref, chosen_ref, blocks_ref, positions_ref, init_v, keys, units, values, cents, held,
     scaled, den, invs, sums, sums_k, sums_v, mass,
     first_a, first_half, first_b, keys_a, vals_a, mass_a, keys_half, vals_half, mass_half,
-    keys_b, vals_b, mass_b, unit_cents, cent_in, parts, fin, att,
+    keys_b, vals_b, mass_b, unit_cents, cent_in, stats, parts, fin_stats, fin, att,
     local_sem, small_sem, k_send, k_recv, v_send, v_recv, a_send, a_recv, b_send, b_recv,
-    g_send, g_recv, c_send, c_recv, f_send, f_recv, o_send, o_recv,
+    g_send, g_recv, c_send, c_recv, s_send, s_recv, f_send, f_recv, o_send, o_recv,
 ):
     heads, tok_dev, dim = key_hbm.shape
     requests, _, group, _ = queries_hbm.shape
@@ -60,7 +60,7 @@
     share = cuts * crow
     owned = share // heads
     tiles = tok_dev // tile
-    pieces, piece_rows = att.shape[1], att.shape[2]
+    half_rows = rows // 2
     me = lax.axis_index("ctx")
     head, core, chip = (me // 2) % heads, me % 2, me // (2 * heads)
     member = chip * 2 + core
@@ -421,9 +421,14 @@
     prob = jnp.where(usable, jnp.exp(score - peak), 0.0).astype(jnp.bfloat16)
     exact_factor = jnp.exp(exact_peak - peak)
     weight_sum = jnp.sum(prob.astype(jnp.float32), axis=1, keepdims=True) + exact_sum * exact_factor
-    shape = (pieces, piece_rows, dim)
-    stat_lanes = lax.broadcasted_iota(jnp.int32, (rows, dim), 1)
-    parts[:, 1] = jnp.where(stat_lanes < dim // 2, weight_sum, peak).reshape(shape)
+    weight_sum = jnp.maximum(weight_sum, 1e-30)
+    log_total = peak + jnp.log(weight_sum)
+    row_lanes = lax.broadcasted_iota(jnp.int32, (half_rows, stats.shape[2]), 1)
+    row_subs = lax.broadcasted_iota(jnp.int32, (half_rows, stats.shape[2]), 0)
+    for side in range(2):
+        here = log_total[side * half_rows : (side + 1) * half_rows]
+        line = jnp.sum(jnp.where(row_lanes == row_subs, here, 0.0), axis=0, keepdims=True)
+        stats[side] = jnp.broadcast_to(line, stats.shape[1:])
     for c in range(cuts):
         for d in range(chips - 1):
             landed(vals_b, 2, d, c)
@@ -431,41 +436,38 @@
     own_values = jnp.concatenate(own_sums[1], axis=0)
     mean_values = (own_values / mass_column).astype(jnp.bfloat16)
     weighted = dot(prob, mean_values, NN) + exact_weighted * exact_factor
-    parts[:, 0] = weighted.reshape(shape)
-
-    def holds(index, action):
-        if pieces == members:
-            action()
-        else:
-            pl.when(index < pieces)(action)
+    parts[...] = (weighted / weight_sum).astype(parts.dtype).reshape(parts.shape)
 
     for d in range(1, members):
         to = (member + d) % members
-
-        def give(to=to, d=d):
-            remote(parts.at[to], fin.at[d], f_send.at[d], f_recv.at[d], at(head, to)).start()
-
-        holds(to, give)
-
-    def finish():
-        for d in range(1, members):
-            remote(parts.at[0], fin.at[d], f_send.at[d], f_recv.at[d], partner).wait_recv()
-        stats = [parts[member]] + [fin[d] for d in range(1, members)]
-        peaks = [stat[1][:, dim - 1 :] for stat in stats]
-        top = functools.reduce(jnp.maximum, peaks)
-        upper, lower = 0.0, 0.0
-        for stat, high in zip(stats, peaks):
-            factor = jnp.exp(high - top)
-            upper = upper + stat[0] * factor
-            lower = lower + stat[1][:, :1] * factor
-        att[head, member] = (upper / lower).astype(jnp.bfloat16)
-        for d in range(1, n):
-            to = (me + d) % n
-            remote(
-                att.at[head, member], att.at[head, member], o_send.at[d], o_recv.at[d], to
-            ).start()
-
-    holds(member, finish)
+        side = to % 2
+        target = at(head, to)
+        begin(stats.at[side], fin_stats.at[d], s_send.at[d], s_recv.at[d], target)
+        begin(parts.at[side], fin.at[d], f_send.at[d], f_recv.at[d], target)
+
+    totals, means = [stats[core]], [parts[core].astype(jnp.float32)]
+    for d in range(1, members):
+        slot = fin_stats.at[d]
+        remote(slot, slot, s_send.at[d], s_recv.at[d], partner).wait_recv()
+        totals.append(fin_stats[d])
+    totals = [
+        jnp.sum(jnp.where(row_lanes == row_subs, total[0:1], 0.0), axis=1, keepdims=True)
+        for total in totals
+    ]
+    top = functools.reduce(jnp.maximum, totals)
+    factors = [jnp.exp(total - top) for total in totals]
+    scale_down = 1.0 / functools.reduce(jnp.add, factors)
+    for d in range(1, members):
+        slot = fin.at[d]
+        remote(slot, slot, f_send.at[d], f_recv.at[d], partner).wait_recv()
+        means.append(fin[d].astype(jnp.float32))
+    upper = functools.reduce(jnp.add, [mean * factor for mean, factor in zip(means, factors)])
+    att[head, core] = (upper * scale_down).astype(jnp.bfloat16)
+    near = [(k, c) for k in range(heads) for c in range(2)][1:]
+    piece = att.at[head, core]
+    for index, (k, c) in enumerate(near):
+        target = at(flipped(head, k), chip * 2 + (core + c) % 2)
+        begin(piece, piece, o_send.at[index], o_recv.at[index], target)
 
     for copy in cent_sends:
         copy.wait_recv()
@@ -474,37 +476,21 @@
         source = flipped(head, k)
         cent_out[source] = cent_in[heads, k]
 
+    per_half = half_rows // group
+
+    def place_out(of_head, side):
+        att_out[pl.ds(side * per_half, per_half), of_head] = (
+            att[of_head, side].astype(jnp.float32).reshape(per_half, group, dim).astype(jnp.bfloat16)
+        )
+
+    place_out(head, core)
+    for index, (k, c) in enumerate(near):
+        source, side = flipped(head, k), (core + c) % 2
+        piece = att.at[source, side]
+        remote(piece, piece, o_send.at[index], o_recv.at[index], partner).wait_recv()
+        place_out(source, side)
     for copy in sent:
         copy.wait_send()
-    for d in range(1, members):
-        to = (member + d) % members
-
-        def gave(to=to, d=d):
-            remote(parts.at[to], fin.at[d], f_send.at[d], f_recv.at[d], at(head, to)).wait_send()
-
-        holds(to, gave)
-
-    for d in range(1, n):
-        source = (me + n - d) % n
-
-        def take(source=source, d=d):
-            piece = att.at[(source // 2) % heads, source // (2 * heads) * 2 + source % 2]
-            remote(piece, piece, o_send.at[d], o_recv.at[d], source).wait_recv()
-
-        holds(source // (2 * heads) * 2 + source % 2, take)
-    per_piece = piece_rows // group
-    for s in range(heads):
-        for p in range(pieces):
-            att_out[p * per_piece : (p + 1) * per_piece, s] = (
-                att[s, p].astype(jnp.float32).reshape(per_piece, group, dim).astype(jnp.bfloat16)
-            )
-
-    def told():
-        piece = att.at[head, member]
-        for d in range(1, n):
-            remote(piece, piece, o_send.at[d], o_recv.at[d], (me + d) % n).wait_send()
-
-    holds(member, told)
 
 
 def put_out(cent_in, att_in, cent_out, att_out, sem):
@@ -537,8 +523,7 @@
     owned = clusters // n
     cuts = 2 if share % 256 == 0 else 1
     crow = share // cuts
-    piece_rows = max(group, requests * group // members)
-    pieces = requests * group // piece_rows
+    half_rows = requests * group // 2
     f32, bf16 = jnp.float32, jnp.bfloat16
     vmem, dma = pltpu.VMEM, pltpu.SemaphoreType.DMA
     anywhere = pl.BlockSpec(memory_space=pl.ANY)
@@ -589,9 +574,11 @@
             vmem(small, f32),
             vmem(whole, bf16),
             vmem((heads + 1, heads, owned, dim), f32),
-            vmem((pieces, 2, piece_rows, dim), f32),
-            vmem((members, 2, piece_rows, dim), f32),
-            vmem((heads, pieces, piece_rows, dim), bf16),
+            vmem((2, 8, 128), f32),
+            vmem((2, half_rows, dim), bf16),
+            vmem((members, 8, 128), f32),
+            vmem((members, half_rows, dim), bf16),
+            vmem((heads, 2, half_rows, dim), bf16),
             dma((3,)),
             dma((4,)),
             dma((heads, tiles)),
@@ -608,8 +595,10 @@
             dma((heads,)),
             dma((members,)),
             dma((members,)),
-            dma((n,)),
-            dma((n,)),
+            dma((members,)),
+            dma((members,)),
+            dma((2 * heads,)),
+            dma((2 * heads,)),
         ],
         compiler_params=pltpu.CompilerParams(
             collective_id=0, has_side_effects=True, vmem_limit_bytes=56 * 1024 * 1024

time: 45.9 us -> 45.2 us (0.985)
  Pallas kernels: 45.1 us -> 44.4 us
    pallas_call x1, Pallas kernels: 44.4 us -> 43.8 us  [body(): pl.pallas_call(functools.partial(kernel, n, tile), out_shape=(vmem((heads...]
where the time goes in v4:
time: 45.2 us; the launch traced here: 45.1 us
  Pallas kernels  44.4 us (98%)
  between operations  0.64 us (1%)
    pallas_call x1, Pallas kernels, body(): pl.pallas_call(functools.partial(kernel, n, tile), out_shape=(vmem((heads...  43.8 us

profile of v4, /device:TPU:0, one launch (start us, length us, event | category | flops | bytes accessed | tf_op | source)
XLA Modules:
  0.0 45.1 jit_solution(1451953602712676761)
XLA Ops:
  0.6 43.8 %shard_map.86 = (f32[4,64,128]{2,1,0:T(8,128)S(1)}, bf16[8,4,8,128]{3,2,1,0:T(8,128)(2,1)S(1)}) custom-call(bf16[4,512,128]{2,1,0:T(8,128)(2,1)} %key_hbm.1, bf16[4,512,128]{2,1,0:T(8,128)(2,1)} %value_hbm.1, bf16[4,1024,128]{2,1,0:T(8,128)(2,1)} %init_hbm.1, bf16[8,4,8,128]{3,2,1,0:T(8,128)(2,1)} %queries_hbm.1, s32[8,4,32]{2,1,0:T(4,128)} %chosen_hbm.1, ...), custom_call_target="tpu_custom_call" | custom-call | tf_op jit(solution)/shard_map/pallas_call | solution.py:537
  44.4 0.7 %shard_map.87 = (f32[4,64,128]{2,1,0:T(8,128)}, bf16[8,4,8,128]{3,2,1,0:T(8,128)(2,1)}) custom-call(f32[4,64,128]{2,1,0:T(8,128)S(1)} %get-tuple-element.4.cent_in, bf16[8,4,8,128]{3,2,1,0:T(8,128)(2,1)S(1)} %get-tuple-element.5.att_in), custom_call_target="tpu_custom_call" | custom-call | tf_op jit(solution)/shard_map/pallas_call | solution.py:616

commit v5 on v4

--- a/solution.py
+++ b/solution.py
@@ -48,7 +48,7 @@
     scaled, den, invs, sums, sums_k, sums_v, mass,
     first_a, first_half, first_b, keys_a, vals_a, mass_a, keys_half, vals_half, mass_half,
     keys_b, vals_b, mass_b, unit_cents, cent_in, stats, parts, fin_stats, fin, att,
-    local_sem, small_sem, k_send, k_recv, v_send, v_recv, a_send, a_recv, b_send, b_recv,
+    local_sem, small_sem, seen_sem, k_send, k_recv, v_send, v_recv, a_send, a_recv, b_send, b_recv,
     g_send, g_recv, c_send, c_recv, s_send, s_recv, f_send, f_recv, o_send, o_recv,
 ):
     heads, tok_dev, dim = key_hbm.shape
@@ -62,20 +62,42 @@
     tiles = tok_dev // tile
     half_rows = rows // 2
     me = lax.axis_index("ctx")
-    head, core, chip = (me // 2) % heads, me % 2, me // (2 * heads)
+    core, chip = me % 2, me // (2 * heads)
+
+    def mirrored(place, of_chip):
+        half = heads // 2
+        return place + (of_chip % 2) * half * (1 - 2 * (place // half % 2))
+
+    head = mirrored((me // 2) % heads, chip)
     member = chip * 2 + core
     other = 1 - core
 
     def at(of_head, of_member):
-        return (of_member // 2) * (2 * heads) + of_head * 2 + of_member % 2
+        of_chip = of_member // 2
+        return of_chip * (2 * heads) + mirrored(of_head, of_chip) * 2 + of_member % 2
 
     barrier = pltpu.get_barrier_semaphore()
     partner = me + 1 - 2 * core
+    near_entry = chips == 2 and heads == 4
     peers = [partner]
-    peers += [at(flipped(head, k), member) for k in range(1, heads)]
-    peers += [at(head, (chip + d) % chips * 2 + core) for d in range(1, chips)]
+    if near_entry:
+        row = me // heads
+        inner = (row == 1) | (row == 2)
+        peers += [at(flipped(head, k), member) for k in (1, 2)]
+    else:
+        peers += [at(flipped(head, k), member) for k in range(1, heads)]
+        peers += [at(head, (chip + d) % chips * 2 + core) for d in range(1, chips)]
+
+    def signal(sem, target):
+        pl.semaphore_signal(sem, inc=1, device_id={"ctx": target}, device_id_type=MESH)
+
     for peer in peers:
-        pl.semaphore_signal(barrier, inc=1, device_id={"ctx": peer}, device_id_type=MESH)
+        signal(barrier, peer)
+    greeted = len(peers)
+    if near_entry:
+        across = at(head, (1 - chip) * 2 + core)
+        pl.when(inner)(lambda: signal(barrier, across))
+        greeted = greeted + jnp.where(inner, 1, 0)
 
     sent = []
 
@@ -107,10 +129,11 @@
     ]
     for copy in small_copies:
         copy.start()
-    pl.semaphore_wait(barrier, len(peers))
+    pl.semaphore_wait(barrier, greeted)
 
     key_sends, value_sends = {}, []
-    for k in range(1, heads):
+
+    def send_keys(k):
         to = flipped(head, k)
         for j in range(tiles):
             span = pl.ds(j * tile, tile)
@@ -119,6 +142,22 @@
                 at(to, member),
             )
 
+    for k in range(1, 3 if near_entry else heads):
+        send_keys(k)
+    if near_entry:
+        signal(seen_sem.at[0], at(flipped(head, 1), member))
+        pl.when(inner)(lambda: signal(seen_sem.at[1], across))
+
+    def send_last_keys():
+        pl.semaphore_wait(seen_sem.at[0], 1)
+        send_keys(3)
+
+        def tell_outer():
+            pl.semaphore_wait(seen_sem.at[1], 1)
+            signal(seen_sem.at[1], at(flipped(head, 2), member))
+
+        pl.when(inner)(tell_outer)
+
     def send_values(k):
         to = flipped(head, k)
         value_sends.append(
@@ -129,7 +168,7 @@
     start = to_unit(init_v[...]).reshape(chips, heads, 2, owned, dim)
     for part in range(members):
         rows_of = jnp.concatenate(
-            [start[part // 2, s, part % 2] for s in range(heads)], axis=0
+            [start[part // 2, mirrored(s, part // 2), part % 2] for s in range(heads)], axis=0
         ).astype(jnp.bfloat16)
         for c in range(cuts):
             cents[part * cuts + c] = rows_of[c * crow : (c + 1) * crow]
@@ -159,6 +198,8 @@
     for k in range(heads):
         for j in range(tiles):
             t = k * tiles + j
+            if near_entry and k == 0 and j == tiles - 1:
+                send_last_keys()
             if k:
                 key_sends[k, j].wait_recv()
             own_keys = keys[k, span_of(j)].astype(jnp.float32)
@@ -187,6 +228,8 @@
         last = block_of(heads - 1)
         return sums[index] + dot(held[index, :, last], scaled[last, :dim], NN)
 
+    if near_entry:
+        pl.when(jnp.logical_not(inner))(lambda: pl.semaphore_wait(seen_sem.at[1], 1))
     first_own = []
     for d in range(chips):
         place = (chip + d + 1) % chips
@@ -484,12 +527,14 @@
         )
 
     place_out(head, core)
+    for copy in sent[: -len(near)]:
+        copy.wait_send()
     for index, (k, c) in enumerate(near):
         source, side = flipped(head, k), (core + c) % 2
         piece = att.at[source, side]
         remote(piece, piece, o_send.at[index], o_recv.at[index], partner).wait_recv()
         place_out(source, side)
-    for copy in sent:
+    for copy in sent[-len(near) :]:
         copy.wait_send()
 
 
@@ -581,6 +626,7 @@
             vmem((heads, 2, half_rows, dim), bf16),
             dma((3,)),
             dma((4,)),
+            pltpu.SemaphoreType.REGULAR((2,)),
             dma((heads, tiles)),
             dma((heads, tiles)),
             dma((heads,)),

time: 45.2 us -> 43.7 us (0.967)
  Pallas kernels: 44.4 us -> 42.9 us
    pallas_call x1, Pallas kernels: 43.8 us -> 42.2 us  [body(): pl.pallas_call(functools.partial(kernel, n, tile), out_shape=(vmem((heads...]
where the time goes in v5:
time: 43.7 us; the launch traced here: 43.6 us
  Pallas kernels  42.9 us (98%)
  between operations  0.64 us (1%)
    pallas_call x1, Pallas kernels, body(): pl.pallas_call(functools.partial(kernel, n, tile), out_shape=(vmem((heads...  42.2 us

profile of v5, /device:TPU:0, one launch (start us, length us, event | category | flops | bytes accessed | tf_op | source)
XLA Modules:
  0.0 43.6 jit_solution(6985747572435766420)
XLA Ops:
  0.6 42.2 %shard_map.86 = (f32[4,64,128]{2,1,0:T(8,128)S(1)}, bf16[8,4,8,128]{3,2,1,0:T(8,128)(2,1)S(1)}) custom-call(bf16[4,512,128]{2,1,0:T(8,128)(2,1)} %key_hbm.1, bf16[4,512,128]{2,1,0:T(8,128)(2,1)} %value_hbm.1, bf16[4,1024,128]{2,1,0:T(8,128)(2,1)} %init_hbm.1, bf16[8,4,8,128]{3,2,1,0:T(8,128)(2,1)} %queries_hbm.1, s32[8,4,32]{2,1,0:T(4,128)} %chosen_hbm.1, ...), custom_call_target="tpu_custom_call" | custom-call | tf_op jit(solution)/shard_map/pallas_call | solution.py:582
  42.9 0.7 %shard_map.87 = (f32[4,64,128]{2,1,0:T(8,128)}, bf16[8,4,8,128]{3,2,1,0:T(8,128)(2,1)}) custom-call(f32[4,64,128]{2,1,0:T(8,128)S(1)} %get-tuple-element.4.cent_in, bf16[8,4,8,128]{3,2,1,0:T(8,128)(2,1)S(1)} %get-tuple-element.5.att_in), custom_call_target="tpu_custom_call" | custom-call | tf_op jit(solution)/shard_map/pallas_call | solution.py:662

commit v6 on v5

--- a/solution.py
+++ b/solution.py
@@ -213,7 +213,7 @@
                 )
                 folds = folded(raised) if folds is None else folds + folded(raised)
             scaled[span_of(t), :dim] = (own_keys * column(inverse(folds))).astype(jnp.bfloat16)
-        if k == 1 and heads > 2:
+        if k == 2 and heads > 2:
             send_values(2)
         if k < heads - 1:
             for index in range(members * cuts):
@@ -364,7 +364,10 @@
             ).astype(jnp.bfloat16)
 
     def second_part(place, side, c):
-        total = dot(held[(place * 2 + side) * cuts + c], scaled[...], NN)
+        index, middle = (place * 2 + side) * cuts + c, heads * tok_dev // 2
+        total = dot(held[index, :, :middle], scaled[:middle], NN) + dot(
+            held[index, :, middle:], scaled[middle:], NN
+        )
         return total[:, :dim], total[:, dim:]
 
     def mass_part(place, side, c):

time: 43.7 us -> 43.5 us (level)
  no operation moved by 1% of the time
where the time goes in v6:
time: 43.5 us; the launch traced here: 43.4 us
  Pallas kernels  42.7 us (98%)
  between operations  0.64 us (1%)
    pallas_call x1, Pallas kernels, body(): pl.pallas_call(functools.partial(kernel, n, tile), out_shape=(vmem((heads...  42.1 us

profile of v6, /device:TPU:0, one launch (start us, length us, event | category | flops | bytes accessed | tf_op | source)
XLA Modules:
  0.0 43.4 jit_solution(8589625050821434343)
XLA Ops:
  0.6 42.1 %shard_map.86 = (f32[4,64,128]{2,1,0:T(8,128)S(1)}, bf16[8,4,8,128]{3,2,1,0:T(8,128)(2,1)S(1)}) custom-call(bf16[4,512,128]{2,1,0:T(8,128)(2,1)} %key_hbm.1, bf16[4,512,128]{2,1,0:T(8,128)(2,1)} %value_hbm.1, bf16[4,1024,128]{2,1,0:T(8,128)(2,1)} %init_hbm.1, bf16[8,4,8,128]{3,2,1,0:T(8,128)(2,1)} %queries_hbm.1, s32[8,4,32]{2,1,0:T(4,128)} %chosen_hbm.1, ...), custom_call_target="tpu_custom_call" | custom-call | tf_op jit(solution)/shard_map/pallas_call | solution.py:585
  42.7 0.7 %shard_map.87 = (f32[4,64,128]{2,1,0:T(8,128)}, bf16[8,4,8,128]{3,2,1,0:T(8,128)(2,1)}) custom-call(f32[4,64,128]{2,1,0:T(8,128)S(1)} %get-tuple-element.4.cent_in, bf16[8,4,8,128]{3,2,1,0:T(8,128)(2,1)S(1)} %get-tuple-element.5.att_in), custom_call_target="tpu_custom_call" | custom-call | tf_op jit(solution)/shard_map/pallas_call | solution.py:665
